TPU v7x, 768 devices: a whole 4x8x12 slice. The times are simulated.
768 devices in a mesh: dp: 64 (over x, y, core), phase: 12 (over z).
Axes of the slice: x: 4, y: 8, z: 12, core: 2. Of those that a mesh axis runs over, the one named last changes fastest.
Arguments:
- patches: bfloat16 [98304, 1280], P(('dp', 'phase')), may hold values from -6 to 6
- window_ids: int32 [768, 128], P(('dp', 'phase')), may hold values from 0 to 3, never falling along the last dimension, each value on 1 to 64 neighbouring positions
- norm_gain: float32 [4, 1280], replicated, may hold values from 0.1 to 1.9
- w_qkv: bfloat16 [4, 1280, 1920], P(None, 'dp')
- w_out: bfloat16 [4, 640, 1280], P(None, 'dp'), may hold values from -0.25 to 0.25
- merge_gain: float32 [1280], replicated, may hold values from 0.1 to 1.9
Outputs:
- merged: bfloat16 [24576, 5120], P(('dp', 'phase'))
Inputs may be any that keep to these rules, and one draw needn't show every extreme that they name: `window_ids`: window numbers never fall along a micro-batch; each window holds 1 to 64 patches, one exactly 64.
All inputs are finite; a program needn't handle non-finite values.
Results may differ from a plain program's by a relative error of at most 0.028.
Values may be sent and summed in bfloat16 or wider, within the bound.
A program may use at most 64 MiB of HBM per device.

v0:
```python
import jax
import jax.numpy as jnp
from jax import lax
from jax.sharding import PartitionSpec as P

D_VIS = 1280
HEADS = 8
HEAD_DIM = 80
SECTIONS = 4


def shifted(block, axis, distance):
    devices = range(lax.axis_size(axis))
    route = [((i - distance) % len(devices), i) for i in devices]
    return lax.ppermute(block, axis, route)


def rms_scale(values, gain):
    return values * lax.rsqrt(jnp.mean(values * values, axis=-1, keepdims=True) + 1e-06) * gain


def finish(acts, gain):
    return rms_scale(acts.astype(jnp.float32), gain).astype(jnp.bfloat16)


def section(acts, marks, gain, weight_qkv, weight_out):
    width = HEADS * HEAD_DIM
    rows = acts.shape[0]
    values_f = acts.astype(jnp.float32)
    normed = rms_scale(values_f, gain).astype(jnp.bfloat16)
    qkv = jnp.dot(normed, weight_qkv, preferred_element_type=jnp.float32).astype(jnp.bfloat16)
    query = qkv[:, :width].reshape(rows, HEADS, HEAD_DIM)
    keys = qkv[:, width : 2 * width].reshape(rows, HEADS, HEAD_DIM)
    vals = qkv[:, 2 * width :].reshape(rows, HEADS, HEAD_DIM)
    scores = jnp.einsum(
        "qhd,khd->hqk", query, keys, preferred_element_type=jnp.float32
    ) * HEAD_DIM ** (-0.5)
    same = marks[:, None] == marks[None, :]
    scores = jnp.where(same[None], scores, jnp.float32(-1e30))
    highest = jnp.max(scores, axis=-1, keepdims=True)
    weights = jnp.exp(scores - highest)
    probs = (weights / jnp.sum(weights, axis=-1, keepdims=True)).astype(jnp.bfloat16)
    context = jnp.einsum("hqk,khd->qhd", probs, vals, preferred_element_type=jnp.float32).astype(
        jnp.bfloat16
    )
    update = jnp.dot(context.reshape(rows, width), weight_out, preferred_element_type=jnp.float32)
    return (values_f + update).astype(jnp.bfloat16)


def body(patches, window_ids, norm_gain, w_qkv, w_out, merge_gain):
    phases = lax.axis_size("phase")
    place = lax.axis_index("phase")
    count = w_qkv.shape[0]
    mine = place % count
    local_qkv = lax.dynamic_index_in_dim(w_qkv, mine, 0, keepdims=False)
    local_out = lax.dynamic_index_in_dim(w_out, mine, 0, keepdims=False)
    weight_qkv, weight_out = (
        lax.all_gather(local_qkv, "dp", axis=0, tiled=True),
        lax.all_gather(local_out, "dp", axis=0, tiled=True),
    )
    gain = lax.dynamic_index_in_dim(norm_gain, mine, 0, keepdims=False)
    marks_start = window_ids[0].astype(jnp.bfloat16)

    def work(step, acts, marks):
        delay = (step - place) % count
        active = step - delay == mine

        def run(values):
            return section(values, marks, gain, weight_qkv, weight_out)

        def keep(values):
            return values

        return lax.cond(active, run, keep, acts)

    laps = (2 * SECTIONS - 2) // phases + 1

    def circle(step, carry):
        acts, marks = carry
        acts = work(step, acts, marks)
        return shifted((acts, marks), "phase", 1)

    acts, marks = lax.fori_loop(0, phases * laps, circle, (patches, marks_start))
    final = finish(acts, merge_gain)
    return final.reshape(-1, 4 * D_VIS)


def solution(mesh):
    in_specs = (
        P(("dp", "phase"), None),
        P(("dp", "phase"), None),
        P(),
        P(None, "dp", None),
        P(None, "dp", None),
        P(),
    )
    out_specs = P(("dp", "phase"), None)
    return jax.shard_map(body, mesh=mesh, in_specs=in_specs, out_specs=out_specs, check_vma=False)
```

profile of v0, /device:TPU:8, one launch (start us, length us, event | category | flops | bytes accessed | tf_op | source)
XLA Modules:
  0.0 394.2 jit_solution(3678643829778576590)
XLA Ops:
  10.5 95.5 %all-gather.7.cloned.1.call-done = bf16[1,640,1280]{2,0,1:T(2,128)(2,1)} async-done(((bf16[1,10,1280]{2,0,1:T(2,128)(2,1)}), bf16[1,640,1280]{2,0,1:T(2,128)(2,1)}) %all-gather.7.cloned.1.call-update) | async-done | bytes 1638416 | tf_op jit(solution)/shard_map/all_gather | solution.py:59
  108.2 96.8 %all-gather.5.cloned.1.call-done = bf16[1,1280,1920]{2,0,1:T(2,128)(2,1)} async-done(((bf16[1,20,1920]{2,0,1:T(2,128)(2,1)}), bf16[1,1280,1920]{2,0,1:T(2,128)(2,1)}) %all-gather.5.cloned.1.call-update) | async-done | bytes 4915216 | tf_op jit(solution)/shard_map/all_gather | solution.py:58
  205.1 6.8 %copy.32 = bf16[1,1280,1920]{2,1,0:T(8,128)(2,1)} copy(bf16[1,1280,1920]{2,0,1:T(2,128)(2,1)} %all-gather.5.cloned.1.call-done) | data formatting | bytes 9830400
  211.9 174.3 %while.20 = (s32[]{:T(128)}, bf16[128,1280]{1,0:T(8,128)(2,1)S(1)}, bf16[128]{0:T(256)(128)(2,1)S(1)}, s32[]{:T(128)}, s32[]{:T(128)}, /*index=5*/f32[1280]{0:T(...) while((s32[]{:T(128)}, bf16[128,1280]{1,0:T(8,128)(2,1)S(1)}, ...), condition=%wide.region_6.7_spmd, body=%wide.region_0.6_spmd.sunk | while | flops 904938880 | bytes 14550152 | solution.py:83
  211.9 5.6 %conditional.2 = (bf16[128,1280]{1,0:T(8,128)(2,1)S(1)}) conditional(s32[]{:T(128)} %convert_element_type.75, bf16[128,1280]{1,0:T(8,128)(2,1)S(1)} %get-tuple-element.312, (bf16[128,1280]{1,0:T(8,128)(2,1)S(1)}, f32[1280]{0:T(1024)S(1)}, bf16[1280,1920]{1,0:T(8,128)(2,1)}, bf16[128]{0:T(256)(128)(2,1)S(1)}, bf16[640,1280]{1,0:T(8,128)(2,1)S(1)}) %tuple.52), branch_computations={%region_1.1_spmd, %region_2.5_spmd} | conditional | flops 904938880 | bytes 12582152 | solution.py:74
  212.1 3.4 convolution_convert_fusion
  221.4 9.1 %collective-permute-done = bf16[128,1280]{1,0:T(8,128)(2,1)S(1)} collective-permute-done((bf16[128,1280]{1,0:T(8,128)(2,1)S(1)}, bf16[128,1280]{1,0:T(8,128)(2,1)S(1)}, u32[]{:S(2)}, u32[]{:S(2)}) %collective-permute-start) | collective-permute-done | bytes 327712 | tf_op jit(solution)/shard_map/while/body/eval_jaxpr/ppermute | solution.py:15
  230.6 5.6 %conditional.2 = (bf16[128,1280]{1,0:T(8,128)(2,1)S(1)}) conditional(s32[]{:T(128)} %convert_element_type.75, bf16[128,1280]{1,0:T(8,128)(2,1)S(1)} %get-tuple-element.312, (bf16[128,1280]{1,0:T(8,128)(2,1)S(1)}, f32[1280]{0:T(1024)S(1)}, bf16[1280,1920]{1,0:T(8,128)(2,1)}, bf16[128]{0:T(256)(128)(2,1)S(1)}, bf16[640,1280]{1,0:T(8,128)(2,1)S(1)}) %tuple.52), branch_computations={%region_1.1_spmd, %region_2.5_spmd} | conditional | flops 904938880 | bytes 12582152 | solution.py:74
  230.8 3.4 convolution_convert_fusion
  240.1 8.3 %collective-permute-done = bf16[128,1280]{1,0:T(8,128)(2,1)S(1)} collective-permute-done((bf16[128,1280]{1,0:T(8,128)(2,1)S(1)}, bf16[128,1280]{1,0:T(8,128)(2,1)S(1)}, u32[]{:S(2)}, u32[]{:S(2)}) %collective-permute-start) | collective-permute-done | bytes 327712 | tf_op jit(solution)/shard_map/while/body/eval_jaxpr/ppermute | solution.py:15
  248.5 5.6 %conditional.2 = (bf16[128,1280]{1,0:T(8,128)(2,1)S(1)}) conditional(s32[]{:T(128)} %convert_element_type.75, bf16[128,1280]{1,0:T(8,128)(2,1)S(1)} %get-tuple-element.312, (bf16[128,1280]{1,0:T(8,128)(2,1)S(1)}, f32[1280]{0:T(1024)S(1)}, bf16[1280,1920]{1,0:T(8,128)(2,1)}, bf16[128]{0:T(256)(128)(2,1)S(1)}, bf16[640,1280]{1,0:T(8,128)(2,1)S(1)}) %tuple.52), branch_computations={%region_1.1_spmd, %region_2.5_spmd} | conditional | flops 904938880 | bytes 12582152 | solution.py:74
  248.7 3.4 convolution_convert_fusion
  258.6 6.8 %collective-permute-done = bf16[128,1280]{1,0:T(8,128)(2,1)S(1)} collective-permute-done((bf16[128,1280]{1,0:T(8,128)(2,1)S(1)}, bf16[128,1280]{1,0:T(8,128)(2,1)S(1)}, u32[]{:S(2)}, u32[]{:S(2)}) %collective-permute-start) | collective-permute-done | bytes 327712 | tf_op jit(solution)/shard_map/while/body/eval_jaxpr/ppermute | solution.py:15
  265.5 5.6 %conditional.2 = (bf16[128,1280]{1,0:T(8,128)(2,1)S(1)}) conditional(s32[]{:T(128)} %convert_element_type.75, bf16[128,1280]{1,0:T(8,128)(2,1)S(1)} %get-tuple-element.312, (bf16[128,1280]{1,0:T(8,128)(2,1)S(1)}, f32[1280]{0:T(1024)S(1)}, bf16[1280,1920]{1,0:T(8,128)(2,1)}, bf16[128]{0:T(256)(128)(2,1)S(1)}, bf16[640,1280]{1,0:T(8,128)(2,1)S(1)}) %tuple.52), branch_computations={%region_1.1_spmd, %region_2.5_spmd} | conditional | flops 904938880 | bytes 12582152 | solution.py:74
  273.0 3.5 collective-permute-start.1
  276.5 4.9 %collective-permute-done = bf16[128,1280]{1,0:T(8,128)(2,1)S(1)} collective-permute-done((bf16[128,1280]{1,0:T(8,128)(2,1)S(1)}, bf16[128,1280]{1,0:T(8,128)(2,1)S(1)}, u32[]{:S(2)}, u32[]{:S(2)}) %collective-permute-start) | collective-permute-done | bytes 327712 | tf_op jit(solution)/shard_map/while/body/eval_jaxpr/ppermute | solution.py:15
  281.5 6.6 %collective-permute-start = (bf16[128,1280]{1,0:T(8,128)(2,1)S(1)}, bf16[128,1280]{1,0:T(8,128)(2,1)S(1)}, u32[]{:S(2)}, u32[]{:S(2)}) collective-permute-start(bf16[128,1280]{1,0:T(8,128)(2,1)S(1)} %get-tuple-element.335), channel_id=1, source_target_pairs={{11,0},{0,1},{1,2},{2,3},{3,4},{4,5},{5,6},{6,7},{7,8},{8,9},{9,10... | collective-permute-start | bytes 983048 | tf_op jit(solution)/shard_map/while/body/eval_jaxpr/ppermute | solution.py:15
  288.1 5.4 %collective-permute-start.1 = (bf16[128]{0:T(256)(128)(2,1)S(1)}, bf16[128]{0:T(256)(128)(2,1)S(1)}, u32[]{:S(2)}, u32[]{:S(2)}) collective-permute-start(bf16[128]{0:T(256)(128)(2,1)S(1)} %copy.41), channel_id=1, source_target_pairs={{11,0},{0,1},{1,2},{2,3},{3,4},{4,5},{5,6},{6,7},{7,8},{8,9},{9,10... | collective-permute-start | bytes 776 | tf_op jit(solution)/shard_map/while/body/eval_jaxpr/ppermute | solution.py:15
  295.1 3.8 collective-permute-start
  298.9 9.7 %collective-permute-start.1 = (bf16[128]{0:T(256)(128)(2,1)S(1)}, bf16[128]{0:T(256)(128)(2,1)S(1)}, u32[]{:S(2)}, u32[]{:S(2)}) collective-permute-start(bf16[128]{0:T(256)(128)(2,1)S(1)} %copy.41), channel_id=1, source_target_pairs={{11,0},{0,1},{1,2},{2,3},{3,4},{4,5},{5,6},{6,7},{7,8},{8,9},{9,10... | collective-permute-start | bytes 776 | tf_op jit(solution)/shard_map/while/body/eval_jaxpr/ppermute | solution.py:15
  309.9 4.8 %collective-permute-start = (bf16[128,1280]{1,0:T(8,128)(2,1)S(1)}, bf16[128,1280]{1,0:T(8,128)(2,1)S(1)}, u32[]{:S(2)}, u32[]{:S(2)}) collective-permute-start(bf16[128,1280]{1,0:T(8,128)(2,1)S(1)} %get-tuple-element.335), channel_id=1, source_target_pairs={{11,0},{0,1},{1,2},{2,3},{3,4},{4,5},{5,6},{6,7},{7,8},{8,9},{9,10... | collective-permute-start | bytes 983048 | tf_op jit(solution)/shard_map/while/body/eval_jaxpr/ppermute | solution.py:15
  314.7 4.4 %collective-permute-start.1 = (bf16[128]{0:T(256)(128)(2,1)S(1)}, bf16[128]{0:T(256)(128)(2,1)S(1)}, u32[]{:S(2)}, u32[]{:S(2)}) collective-permute-start(bf16[128]{0:T(256)(128)(2,1)S(1)} %copy.41), channel_id=1, source_target_pairs={{11,0},{0,1},{1,2},{2,3},{3,4},{4,5},{5,6},{6,7},{7,8},{8,9},{9,10... | collective-permute-start | bytes 776 | tf_op jit(solution)/shard_map/while/body/eval_jaxpr/ppermute | solution.py:15
  319.1 5.9 %collective-permute-done = bf16[128,1280]{1,0:T(8,128)(2,1)S(1)} collective-permute-done((bf16[128,1280]{1,0:T(8,128)(2,1)S(1)}, bf16[128,1280]{1,0:T(8,128)(2,1)S(1)}, u32[]{:S(2)}, u32[]{:S(2)}) %collective-permute-start) | collective-permute-done | bytes 327712 | tf_op jit(solution)/shard_map/while/body/eval_jaxpr/ppermute | solution.py:15
  328.3 5.7 %collective-permute-start.1 = (bf16[128]{0:T(256)(128)(2,1)S(1)}, bf16[128]{0:T(256)(128)(2,1)S(1)}, u32[]{:S(2)}, u32[]{:S(2)}) collective-permute-start(bf16[128]{0:T(256)(128)(2,1)S(1)} %copy.41), channel_id=1, source_target_pairs={{11,0},{0,1},{1,2},{2,3},{3,4},{4,5},{5,6},{6,7},{7,8},{8,9},{9,10... | collective-permute-start | bytes 776 | tf_op jit(solution)/shard_map/while/body/eval_jaxpr/ppermute | solution.py:15
  336.5 5.3 %collective-permute-start = (bf16[128,1280]{1,0:T(8,128)(2,1)S(1)}, bf16[128,1280]{1,0:T(8,128)(2,1)S(1)}, u32[]{:S(2)}, u32[]{:S(2)}) collective-permute-start(bf16[128,1280]{1,0:T(8,128)(2,1)S(1)} %get-tuple-element.335), channel_id=1, source_target_pairs={{11,0},{0,1},{1,2},{2,3},{3,4},{4,5},{5,6},{6,7},{7,8},{8,9},{9,10... | collective-permute-start | bytes 983048 | tf_op jit(solution)/shard_map/while/body/eval_jaxpr/ppermute | solution.py:15
  341.8 4.7 %collective-permute-start.1 = (bf16[128]{0:T(256)(128)(2,1)S(1)}, bf16[128]{0:T(256)(128)(2,1)S(1)}, u32[]{:S(2)}, u32[]{:S(2)}) collective-permute-start(bf16[128]{0:T(256)(128)(2,1)S(1)} %copy.41), channel_id=1, source_target_pairs={{11,0},{0,1},{1,2},{2,3},{3,4},{4,5},{5,6},{6,7},{7,8},{8,9},{9,10... | collective-permute-start | bytes 776 | tf_op jit(solution)/shard_map/while/body/eval_jaxpr/ppermute | solution.py:15
  349.5 4.4 %collective-permute-start = (bf16[128,1280]{1,0:T(8,128)(2,1)S(1)}, bf16[128,1280]{1,0:T(8,128)(2,1)S(1)}, u32[]{:S(2)}, u32[]{:S(2)}) collective-permute-start(bf16[128,1280]{1,0:T(8,128)(2,1)S(1)} %get-tuple-element.335), channel_id=1, source_target_pairs={{11,0},{0,1},{1,2},{2,3},{3,4},{4,5},{5,6},{6,7},{7,8},{8,9},{9,10... | collective-permute-start | bytes 983048 | tf_op jit(solution)/shard_map/while/body/eval_jaxpr/ppermute | solution.py:15
  354.0 4.4 %collective-permute-start.1 = (bf16[128]{0:T(256)(128)(2,1)S(1)}, bf16[128]{0:T(256)(128)(2,1)S(1)}, u32[]{:S(2)}, u32[]{:S(2)}) collective-permute-start(bf16[128]{0:T(256)(128)(2,1)S(1)} %copy.41), channel_id=1, source_target_pairs={{11,0},{0,1},{1,2},{2,3},{3,4},{4,5},{5,6},{6,7},{7,8},{8,9},{9,10... | collective-permute-start | bytes 776 | tf_op jit(solution)/shard_map/while/body/eval_jaxpr/ppermute | solution.py:15
  358.4 4.7 %collective-permute-done = bf16[128,1280]{1,0:T(8,128)(2,1)S(1)} collective-permute-done((bf16[128,1280]{1,0:T(8,128)(2,1)S(1)}, bf16[128,1280]{1,0:T(8,128)(2,1)S(1)}, u32[]{:S(2)}, u32[]{:S(2)}) %collective-permute-start) | collective-permute-done | bytes 327712 | tf_op jit(solution)/shard_map/while/body/eval_jaxpr/ppermute | solution.py:15
  365.2 4.1 %collective-permute-start.1 = (bf16[128]{0:T(256)(128)(2,1)S(1)}, bf16[128]{0:T(256)(128)(2,1)S(1)}, u32[]{:S(2)}, u32[]{:S(2)}) collective-permute-start(bf16[128]{0:T(256)(128)(2,1)S(1)} %copy.41), channel_id=1, source_target_pairs={{11,0},{0,1},{1,2},{2,3},{3,4},{4,5},{5,6},{6,7},{7,8},{8,9},{9,10... | collective-permute-start | bytes 776 | tf_op jit(solution)/shard_map/while/body/eval_jaxpr/ppermute | solution.py:15
  369.4 6.4 %collective-permute-done = bf16[128,1280]{1,0:T(8,128)(2,1)S(1)} collective-permute-done((bf16[128,1280]{1,0:T(8,128)(2,1)S(1)}, bf16[128,1280]{1,0:T(8,128)(2,1)S(1)}, u32[]{:S(2)}, u32[]{:S(2)}) %collective-permute-start) | collective-permute-done | bytes 327712 | tf_op jit(solution)/shard_map/while/body/eval_jaxpr/ppermute | solution.py:15
  380.7 5.4 %collective-permute-done = bf16[128,1280]{1,0:T(8,128)(2,1)S(1)} collective-permute-done((bf16[128,1280]{1,0:T(8,128)(2,1)S(1)}, bf16[128,1280]{1,0:T(8,128)(2,1)S(1)}, u32[]{:S(2)}, u32[]{:S(2)}) %collective-permute-start) | collective-permute-done | bytes 327712 | tf_op jit(solution)/shard_map/while/body/eval_jaxpr/ppermute | solution.py:15
  (123 shorter events, 52.5 us)
Async XLA Ops:
  6.5 1.7 copy-start
  6.5 99.5 %all-gather.7.cloned.1.call-start = ((), (), s32[]{:S(2)}) async-start(), calls=%async_computation.1 | async-start | bytes 3328000 | tf_op jit(solution)/shard_map/all_gather | solution.py:59
  8.2 196.9 %all-gather.5.cloned.1.call-start = ((), (), s32[]{:S(2)}) async-start(), calls=%async_computation | async-start | bytes 9984000 | tf_op jit(solution)/shard_map/all_gather | solution.py:58
  108.2 103.7 %copy-start.1 = (bf16[128,1280]{1,0:T(8,128)(2,1)S(1)}, bf16[128,1280]{1,0:T(8,128)(2,1)}, u32[]{:S(2)}) copy-start(bf16[128,1280]{1,0:T(8,128)(2,1)} %param.10) | copy-start | bytes 983044
  211.9 174.4 %copy-start.2 = (f32[1280]{0:T(1024)S(1)}, f32[1280]{0:T(1024)}, u32[]{:S(2)}) copy-start(f32[1280]{0:T(1024)} %param.15) | copy-start | bytes 15364
  217.5 13.0 %collective-permute-start = (bf16[128,1280]{1,0:T(8,128)(2,1)S(1)}, bf16[128,1280]{1,0:T(8,128)(2,1)S(1)}, u32[]{:S(2)}, u32[]{:S(2)}) collective-permute-start(bf16[128,1280]{1,0:T(8,128)(2,1)S(1)} %get-tuple-element.335), channel_id=1, source_target_pairs={{11,0},{0,1},{1,2},{2,3},{3,4},{4,5},{5,6},{6,7},{7,8},{8,9},{9,10... | collective-permute-start | bytes 983048 | tf_op jit(solution)/shard_map/while/body/eval_jaxpr/ppermute | solution.py:15
  219.5 11.1 %collective-permute-start.1 = (bf16[128]{0:T(256)(128)(2,1)S(1)}, bf16[128]{0:T(256)(128)(2,1)S(1)}, u32[]{:S(2)}, u32[]{:S(2)}) collective-permute-start(bf16[128]{0:T(256)(128)(2,1)S(1)} %copy.41), channel_id=1, source_target_pairs={{11,0},{0,1},{1,2},{2,3},{3,4},{4,5},{5,6},{6,7},{7,8},{8,9},{9,10... | collective-permute-start | bytes 776 | tf_op jit(solution)/shard_map/while/body/eval_jaxpr/ppermute | solution.py:15
  236.2 12.2 %collective-permute-start = (bf16[128,1280]{1,0:T(8,128)(2,1)S(1)}, bf16[128,1280]{1,0:T(8,128)(2,1)S(1)}, u32[]{:S(2)}, u32[]{:S(2)}) collective-permute-start(bf16[128,1280]{1,0:T(8,128)(2,1)S(1)} %get-tuple-element.335), channel_id=1, source_target_pairs={{11,0},{0,1},{1,2},{2,3},{3,4},{4,5},{5,6},{6,7},{7,8},{8,9},{9,10... | collective-permute-start | bytes 983048 | tf_op jit(solution)/shard_map/while/body/eval_jaxpr/ppermute | solution.py:15
  238.2 10.3 %collective-permute-start.1 = (bf16[128]{0:T(256)(128)(2,1)S(1)}, bf16[128]{0:T(256)(128)(2,1)S(1)}, u32[]{:S(2)}, u32[]{:S(2)}) collective-permute-start(bf16[128]{0:T(256)(128)(2,1)S(1)} %copy.41), channel_id=1, source_target_pairs={{11,0},{0,1},{1,2},{2,3},{3,4},{4,5},{5,6},{6,7},{7,8},{8,9},{9,10... | collective-permute-start | bytes 776 | tf_op jit(solution)/shard_map/while/body/eval_jaxpr/ppermute | solution.py:15
  254.1 11.2 %collective-permute-start = (bf16[128,1280]{1,0:T(8,128)(2,1)S(1)}, bf16[128,1280]{1,0:T(8,128)(2,1)S(1)}, u32[]{:S(2)}, u32[]{:S(2)}) collective-permute-start(bf16[128,1280]{1,0:T(8,128)(2,1)S(1)} %get-tuple-element.335), channel_id=1, source_target_pairs={{11,0},{0,1},{1,2},{2,3},{3,4},{4,5},{5,6},{6,7},{7,8},{8,9},{9,10... | collective-permute-start | bytes 983048 | tf_op jit(solution)/shard_map/while/body/eval_jaxpr/ppermute | solution.py:15
  256.1 9.4 %collective-permute-start.1 = (bf16[128]{0:T(256)(128)(2,1)S(1)}, bf16[128]{0:T(256)(128)(2,1)S(1)}, u32[]{:S(2)}, u32[]{:S(2)}) collective-permute-start(bf16[128]{0:T(256)(128)(2,1)S(1)} %copy.41), channel_id=1, source_target_pairs={{11,0},{0,1},{1,2},{2,3},{3,4},{4,5},{5,6},{6,7},{7,8},{8,9},{9,10... | collective-permute-start | bytes 776 | tf_op jit(solution)/shard_map/while/body/eval_jaxpr/ppermute | solution.py:15
  271.1 10.3 %collective-permute-start = (bf16[128,1280]{1,0:T(8,128)(2,1)S(1)}, bf16[128,1280]{1,0:T(8,128)(2,1)S(1)}, u32[]{:S(2)}, u32[]{:S(2)}) collective-permute-start(bf16[128,1280]{1,0:T(8,128)(2,1)S(1)} %get-tuple-element.335), channel_id=1, source_target_pairs={{11,0},{0,1},{1,2},{2,3},{3,4},{4,5},{5,6},{6,7},{7,8},{8,9},{9,10... | collective-permute-start | bytes 983048 | tf_op jit(solution)/shard_map/while/body/eval_jaxpr/ppermute | solution.py:15
  273.0 8.4 %collective-permute-start.1 = (bf16[128]{0:T(256)(128)(2,1)S(1)}, bf16[128]{0:T(256)(128)(2,1)S(1)}, u32[]{:S(2)}, u32[]{:S(2)}) collective-permute-start(bf16[128]{0:T(256)(128)(2,1)S(1)} %copy.41), channel_id=1, source_target_pairs={{11,0},{0,1},{1,2},{2,3},{3,4},{4,5},{5,6},{6,7},{7,8},{8,9},{9,10... | collective-permute-start | bytes 776 | tf_op jit(solution)/shard_map/while/body/eval_jaxpr/ppermute | solution.py:15
  281.5 13.5 %collective-permute-start = (bf16[128,1280]{1,0:T(8,128)(2,1)S(1)}, bf16[128,1280]{1,0:T(8,128)(2,1)S(1)}, u32[]{:S(2)}, u32[]{:S(2)}) collective-permute-start(bf16[128,1280]{1,0:T(8,128)(2,1)S(1)} %get-tuple-element.335), channel_id=1, source_target_pairs={{11,0},{0,1},{1,2},{2,3},{3,4},{4,5},{5,6},{6,7},{7,8},{8,9},{9,10... | collective-permute-start | bytes 983048 | tf_op jit(solution)/shard_map/while/body/eval_jaxpr/ppermute | solution.py:15
  288.1 7.0 %collective-permute-start.1 = (bf16[128]{0:T(256)(128)(2,1)S(1)}, bf16[128]{0:T(256)(128)(2,1)S(1)}, u32[]{:S(2)}, u32[]{:S(2)}) collective-permute-start(bf16[128]{0:T(256)(128)(2,1)S(1)} %copy.41), channel_id=1, source_target_pairs={{11,0},{0,1},{1,2},{2,3},{3,4},{4,5},{5,6},{6,7},{7,8},{8,9},{9,10... | collective-permute-start | bytes 776 | tf_op jit(solution)/shard_map/while/body/eval_jaxpr/ppermute | solution.py:15
  295.1 14.6 %collective-permute-start = (bf16[128,1280]{1,0:T(8,128)(2,1)S(1)}, bf16[128,1280]{1,0:T(8,128)(2,1)S(1)}, u32[]{:S(2)}, u32[]{:S(2)}) collective-permute-start(bf16[128,1280]{1,0:T(8,128)(2,1)S(1)} %get-tuple-element.335), channel_id=1, source_target_pairs={{11,0},{0,1},{1,2},{2,3},{3,4},{4,5},{5,6},{6,7},{7,8},{8,9},{9,10... | collective-permute-start | bytes 983048 | tf_op jit(solution)/shard_map/while/body/eval_jaxpr/ppermute | solution.py:15
  298.9 11.0 %collective-permute-start.1 = (bf16[128]{0:T(256)(128)(2,1)S(1)}, bf16[128]{0:T(256)(128)(2,1)S(1)}, u32[]{:S(2)}, u32[]{:S(2)}) collective-permute-start(bf16[128]{0:T(256)(128)(2,1)S(1)} %copy.41), channel_id=1, source_target_pairs={{11,0},{0,1},{1,2},{2,3},{3,4},{4,5},{5,6},{6,7},{7,8},{8,9},{9,10... | collective-permute-start | bytes 776 | tf_op jit(solution)/shard_map/while/body/eval_jaxpr/ppermute | solution.py:15
  309.9 15.1 %collective-permute-start = (bf16[128,1280]{1,0:T(8,128)(2,1)S(1)}, bf16[128,1280]{1,0:T(8,128)(2,1)S(1)}, u32[]{:S(2)}, u32[]{:S(2)}) collective-permute-start(bf16[128,1280]{1,0:T(8,128)(2,1)S(1)} %get-tuple-element.335), channel_id=1, source_target_pairs={{11,0},{0,1},{1,2},{2,3},{3,4},{4,5},{5,6},{6,7},{7,8},{8,9},{9,10... | collective-permute-start | bytes 983048 | tf_op jit(solution)/shard_map/while/body/eval_jaxpr/ppermute | solution.py:15
  314.7 10.3 %collective-permute-start.1 = (bf16[128]{0:T(256)(128)(2,1)S(1)}, bf16[128]{0:T(256)(128)(2,1)S(1)}, u32[]{:S(2)}, u32[]{:S(2)}) collective-permute-start(bf16[128]{0:T(256)(128)(2,1)S(1)} %copy.41), channel_id=1, source_target_pairs={{11,0},{0,1},{1,2},{2,3},{3,4},{4,5},{5,6},{6,7},{7,8},{8,9},{9,10... | collective-permute-start | bytes 776 | tf_op jit(solution)/shard_map/while/body/eval_jaxpr/ppermute | solution.py:15
  325.1 11.3 %collective-permute-start = (bf16[128,1280]{1,0:T(8,128)(2,1)S(1)}, bf16[128,1280]{1,0:T(8,128)(2,1)S(1)}, u32[]{:S(2)}, u32[]{:S(2)}) collective-permute-start(bf16[128,1280]{1,0:T(8,128)(2,1)S(1)} %get-tuple-element.335), channel_id=1, source_target_pairs={{11,0},{0,1},{1,2},{2,3},{3,4},{4,5},{5,6},{6,7},{7,8},{8,9},{9,10... | collective-permute-start | bytes 983048 | tf_op jit(solution)/shard_map/while/body/eval_jaxpr/ppermute | solution.py:15
  328.3 8.2 %collective-permute-start.1 = (bf16[128]{0:T(256)(128)(2,1)S(1)}, bf16[128]{0:T(256)(128)(2,1)S(1)}, u32[]{:S(2)}, u32[]{:S(2)}) collective-permute-start(bf16[128]{0:T(256)(128)(2,1)S(1)} %copy.41), channel_id=1, source_target_pairs={{11,0},{0,1},{1,2},{2,3},{3,4},{4,5},{5,6},{6,7},{7,8},{8,9},{9,10... | collective-permute-start | bytes 776 | tf_op jit(solution)/shard_map/while/body/eval_jaxpr/ppermute | solution.py:15
  336.5 12.9 %collective-permute-start = (bf16[128,1280]{1,0:T(8,128)(2,1)S(1)}, bf16[128,1280]{1,0:T(8,128)(2,1)S(1)}, u32[]{:S(2)}, u32[]{:S(2)}) collective-permute-start(bf16[128,1280]{1,0:T(8,128)(2,1)S(1)} %get-tuple-element.335), channel_id=1, source_target_pairs={{11,0},{0,1},{1,2},{2,3},{3,4},{4,5},{5,6},{6,7},{7,8},{8,9},{9,10... | collective-permute-start | bytes 983048 | tf_op jit(solution)/shard_map/while/body/eval_jaxpr/ppermute | solution.py:15
  341.8 7.6 %collective-permute-start.1 = (bf16[128]{0:T(256)(128)(2,1)S(1)}, bf16[128]{0:T(256)(128)(2,1)S(1)}, u32[]{:S(2)}, u32[]{:S(2)}) collective-permute-start(bf16[128]{0:T(256)(128)(2,1)S(1)} %copy.41), channel_id=1, source_target_pairs={{11,0},{0,1},{1,2},{2,3},{3,4},{4,5},{5,6},{6,7},{7,8},{8,9},{9,10... | collective-permute-start | bytes 776 | tf_op jit(solution)/shard_map/while/body/eval_jaxpr/ppermute | solution.py:15
  349.5 13.5 %collective-permute-start = (bf16[128,1280]{1,0:T(8,128)(2,1)S(1)}, bf16[128,1280]{1,0:T(8,128)(2,1)S(1)}, u32[]{:S(2)}, u32[]{:S(2)}) collective-permute-start(bf16[128,1280]{1,0:T(8,128)(2,1)S(1)} %get-tuple-element.335), channel_id=1, source_target_pairs={{11,0},{0,1},{1,2},{2,3},{3,4},{4,5},{5,6},{6,7},{7,8},{8,9},{9,10... | collective-permute-start | bytes 983048 | tf_op jit(solution)/shard_map/while/body/eval_jaxpr/ppermute | solution.py:15
  354.0 9.1 %collective-permute-start.1 = (bf16[128]{0:T(256)(128)(2,1)S(1)}, bf16[128]{0:T(256)(128)(2,1)S(1)}, u32[]{:S(2)}, u32[]{:S(2)}) collective-permute-start(bf16[128]{0:T(256)(128)(2,1)S(1)} %copy.41), channel_id=1, source_target_pairs={{11,0},{0,1},{1,2},{2,3},{3,4},{4,5},{5,6},{6,7},{7,8},{8,9},{9,10... | collective-permute-start | bytes 776 | tf_op jit(solution)/shard_map/while/body/eval_jaxpr/ppermute | solution.py:15
  363.1 12.7 %collective-permute-start = (bf16[128,1280]{1,0:T(8,128)(2,1)S(1)}, bf16[128,1280]{1,0:T(8,128)(2,1)S(1)}, u32[]{:S(2)}, u32[]{:S(2)}) collective-permute-start(bf16[128,1280]{1,0:T(8,128)(2,1)S(1)} %get-tuple-element.335), channel_id=1, source_target_pairs={{11,0},{0,1},{1,2},{2,3},{3,4},{4,5},{5,6},{6,7},{7,8},{8,9},{9,10... | collective-permute-start | bytes 983048 | tf_op jit(solution)/shard_map/while/body/eval_jaxpr/ppermute | solution.py:15
  365.2 10.7 %collective-permute-start.1 = (bf16[128]{0:T(256)(128)(2,1)S(1)}, bf16[128]{0:T(256)(128)(2,1)S(1)}, u32[]{:S(2)}, u32[]{:S(2)}) collective-permute-start(bf16[128]{0:T(256)(128)(2,1)S(1)} %copy.41), channel_id=1, source_target_pairs={{11,0},{0,1},{1,2},{2,3},{3,4},{4,5},{5,6},{6,7},{7,8},{8,9},{9,10... | collective-permute-start | bytes 776 | tf_op jit(solution)/shard_map/while/body/eval_jaxpr/ppermute | solution.py:15
  375.9 10.2 %collective-permute-start = (bf16[128,1280]{1,0:T(8,128)(2,1)S(1)}, bf16[128,1280]{1,0:T(8,128)(2,1)S(1)}, u32[]{:S(2)}, u32[]{:S(2)}) collective-permute-start(bf16[128,1280]{1,0:T(8,128)(2,1)S(1)} %get-tuple-element.335), channel_id=1, source_target_pairs={{11,0},{0,1},{1,2},{2,3},{3,4},{4,5},{5,6},{6,7},{7,8},{8,9},{9,10... | collective-permute-start | bytes 983048 | tf_op jit(solution)/shard_map/while/body/eval_jaxpr/ppermute | solution.py:15
  377.8 8.3 %collective-permute-start.1 = (bf16[128]{0:T(256)(128)(2,1)S(1)}, bf16[128]{0:T(256)(128)(2,1)S(1)}, u32[]{:S(2)}, u32[]{:S(2)}) collective-permute-start(bf16[128]{0:T(256)(128)(2,1)S(1)} %copy.41), channel_id=1, source_target_pairs={{11,0},{0,1},{1,2},{2,3},{3,4},{4,5},{5,6},{6,7},{7,8},{8,9},{9,10... | collective-permute-start | bytes 776 | tf_op jit(solution)/shard_map/while/body/eval_jaxpr/ppermute | solution.py:15
Sparse Core Ops, SparseCore 0:
  11.2 94.7 all-gather.6
  110.0 95.0 all-gather.4
where the time goes:
time: 395 us; the launch traced here: 394 us
  waiting for transfers between devices  252 us (64%)
  starting transfers between devices  90.9 us (23%)
  matrix products  19.1 us (5%)
  local copies, waits for them, and re-layouts  15.6 us (4%)
  between operations  13.4 us (3%)
    all_gather x1, waiting for transfers between devices, body(): lax.all_gather(local_qkv, 'dp', axis=0, tiled=True)  96.8 us
    all_gather x1, waiting for transfers between devices, body(): lax.all_gather(local_out, 'dp', axis=0, tiled=True)  95.5 us
    ppermute x24, starting transfers between devices, shifted(): return lax.ppermute(block, axis, route)  90.9 us
    ppermute x24, waiting for transfers between devices, shifted(): return lax.ppermute(block, axis, route)  59.9 us
    dot_general x4, matrix products, section(): jnp.dot(normed, weight_qkv, preferred_element_type=jnp.float32)  13.4 us
    unnamed x8, local copies, waits for them, and re-layouts  9 us
  transfers between devices with their start and end apart: 26, of which 15 were waited for; matrix products, arithmetic and copies ran while one was open for 1% of the time, Pallas kernels for 0%

commit v1 on v0

v1 whole, which is shorter than its diff:
```python
import jax
import jax.numpy as jnp
from jax import lax
from jax.experimental import pallas as pl
from jax.experimental.pallas import tpu as pltpu
from jax.sharding import PartitionSpec as P

D_VIS = 1280
HEADS = 8
HEAD_DIM = 80
WIDTH = HEADS * HEAD_DIM
MB = 128
SECTIONS = 4
NX, NY = 4, 8
ROWS = 40
CA, CB = 384, 512
STEPS = 10
LAG = 2
MESH = pl.DeviceIdType.MESH


def rms(values, gain):
    return values * lax.rsqrt(jnp.mean(values * values, axis=-1, keepdims=True) + 1e-06) * gain


def kernel(
    block_a, block_b, patches, ids, gains, merge_gain, spread, out,
    wa, wb, acts, ctx, mask, tail,
    local_sem, ax, ay, az, by, bx, sib_a, sib_z, sib_b, sent,
):
    dp, z = lax.axis_index("dp"), lax.axis_index("phase")
    planes = lax.axis_size("phase")
    core = lax.rem(dp, 2)
    x, y = lax.div(dp, 2 * NY), lax.rem(lax.div(dp, 2), NY)
    half = lax.rem(z, 2)
    side = 1 - 2 * core

    def place(px, py, pc):
        return ((px * NY + py) * 2 + pc, z)

    def xs(d):
        return lax.rem(x + d + NX, NX)

    def ys(d):
        return lax.rem(y + d + NY, NY)

    east, west = place(xs(1), y, core), place(xs(-1), y, core)
    north, south = place(x, ys(1), core), place(x, ys(-1), core)
    up = (dp, lax.rem(z + 1, planes))
    down = (dp, lax.rem(z + planes - 1, planes))
    twin = place(x, y, 1 - core)
    x_side, y_side = place(xs(side), y, core), place(x, ys(side), core)

    def copy(ref, kind, recv, device):
        return pltpu.make_async_remote_copy(
            src_ref=ref, dst_ref=ref, send_sem=sent.at[kind], recv_sem=recv,
            device_id=device, device_id_type=MESH,
        )

    def send(ref, kind, recv, device):
        copy(ref, kind, recv, device).start()

    def arrive(ref, recv):
        copy(ref, 0, recv, twin).wait_recv()

    def drain(ref, kind):
        copy(ref, kind, local_sem.at[2], twin).wait_send()

    own_a = pltpu.make_async_copy(block_a.at[:, half], wa.at[core, :, half, x, y], local_sem.at[0])
    own_b = pltpu.make_async_copy(block_b, wb.at[core, :, x, y], local_sem.at[1])
    for item in (own_a, own_b):
        item.start()
    barrier = pltpu.get_barrier_semaphore()
    for device in (east, west, north, south, up, down, twin):
        pl.semaphore_signal(barrier, inc=1, device_id=device, device_id_type=MESH)

    marks = jnp.broadcast_to(ids[...].astype(jnp.float32), (MB, MB))
    mask[...] = jnp.where(marks == marks.T, jnp.float32(1), jnp.float32(0))
    acts[...] = patches[...]

    pl.semaphore_wait(barrier, 7)
    for item in (own_a, own_b):
        item.wait()

    def row_a(s, py):
        return wa.at[core, s, half, :, py]

    def spread_row(s, py):
        send(wa.at[core, s, half, 0:2, py], 2, az.at[s, 0], up)
        send(wa.at[core, s, half, 2:4, py], 2, az.at[s, 1], down)
        send(row_a(s, py), 3, sib_a.at[s], twin)

    def step_a(s, k):
        if k == 0:
            mine = wa.at[core, s, half, x, y]
            send(mine, 0, ax.at[s, 0], east)
            send(mine, 0, ax.at[s, 1], west)
        elif k == 1:
            arrive(wa.at[core, s, half, xs(-1), y], ax.at[s, 0])
            arrive(wa.at[core, s, half, xs(1), y], ax.at[s, 1])
            send(wa.at[core, s, half, xs(-side), y], 0, ax.at[s, 2], x_side)
        elif k == 2:
            arrive(wa.at[core, s, half, xs(2), y], ax.at[s, 2])
            send(row_a(s, y), 1, ay.at[s, 0], north)
            send(row_a(s, y), 1, ay.at[s, 1], south)
            spread_row(s, y)
        elif k in (3, 4, 5):
            d = k - 2
            arrive(row_a(s, ys(-d)), ay.at[s, 2 * d - 2])
            arrive(row_a(s, ys(d)), ay.at[s, 2 * d - 1])
            if d < 3:
                send(row_a(s, ys(-d)), 1, ay.at[s, 2 * d], north)
                send(row_a(s, ys(d)), 1, ay.at[s, 2 * d + 1], south)
            else:
                send(row_a(s, ys(-3 * side)), 1, ay.at[s, 6], y_side)
            spread_row(s, ys(-d))
            spread_row(s, ys(d))
        elif k == 6:
            arrive(row_a(s, ys(4)), ay.at[s, 6])
            spread_row(s, ys(4))
        elif k == 8:
            arrive(wa.at[core, s, 1 - half, 0:2], az.at[s, 0])
            arrive(wa.at[core, s, 1 - half, 2:4], az.at[s, 1])
            send(wa.at[core, s, 1 - half], 4, sib_z.at[s], twin)
        elif k == 9:
            arrive(wa.at[1 - core, s, half], sib_a.at[s])
            arrive(wa.at[1 - core, s, 1 - half], sib_z.at[s])

    def step_b(s, k):
        if k == 0:
            mine = wb.at[core, s, x, y]
            send(mine, 5, by.at[s, 0], north)
            send(mine, 5, by.at[s, 1], south)
        elif k in (1, 2, 3):
            d = k
            arrive(wb.at[core, s, x, ys(-d)], by.at[s, 2 * d - 2])
            arrive(wb.at[core, s, x, ys(d)], by.at[s, 2 * d - 1])
            if d < 3:
                send(wb.at[core, s, x, ys(-d)], 5, by.at[s, 2 * d], north)
                send(wb.at[core, s, x, ys(d)], 5, by.at[s, 2 * d + 1], south)
            else:
                send(wb.at[core, s, x, ys(-3 * side)], 5, by.at[s, 6], y_side)
        elif k == 4:
            arrive(wb.at[core, s, x, ys(4)], by.at[s, 6])
            send(wb.at[core, s, x], 6, bx.at[s, 0], east)
            send(wb.at[core, s, x], 6, bx.at[s, 1], west)
            send(wb.at[core, s, x], 7, sib_b.at[s], twin)
        elif k == 6:
            arrive(wb.at[core, s, xs(-1)], bx.at[s, 0])
            arrive(wb.at[core, s, xs(1)], bx.at[s, 1])
            send(wb.at[core, s, xs(-side)], 6, bx.at[s, 2], x_side)
            send(wb.at[core, s, xs(-1)], 7, sib_b.at[s], twin)
            send(wb.at[core, s, xs(1)], 7, sib_b.at[s], twin)
        elif k == 8:
            arrive(wb.at[core, s, xs(2)], bx.at[s, 2])
            send(wb.at[core, s, xs(2)], 7, sib_b.at[s], twin)
        elif k == 9:
            arrive(wb.at[1 - core, s], sib_b.at[s])

    for tick in range(LAG * (SECTIONS - 1) + STEPS):
        for s in range(SECTIONS):
            k = tick - LAG * s
            if 0 <= k < STEPS:
                step_a(s, k)
                step_b(s, k)

    drain(wa.at[0, :, 0, 0:3, 0], 0)
    drain(wa.at[0, :, 0, :, 0:7], 1)
    drain(wa.at[0, :, 0], 2)
    drain(wa.at[0, :, 0], 3)
    drain(wa.at[0, :, 0], 4)
    drain(wb.at[0, :, 0, 0:7], 5)
    drain(wb.at[0, :, 0:3], 6)
    drain(wb.at[0], 7)

    def weight_a(lane, s, h):
        return wa[lane, s, h].reshape(D_VIS, CA)

    def weight_b(lane, s):
        return wb[lane, s].reshape(D_VIS, CB)

    def dot(a, b):
        return jnp.dot(a, b, preferred_element_type=jnp.float32)

    lanes = lax.broadcasted_iota(jnp.int32, (1, 256), 1)

    def section(s, carry):
        values = acts[...].astype(jnp.float32)
        normed = rms(values, gains[pl.ds(s, 1), :]).astype(jnp.bfloat16)
        qk = [
            dot(normed, weight_a(0, s, 0)), dot(normed, weight_a(0, s, 1)), dot(normed, weight_b(0, s)),
        ]
        qk = jnp.concatenate([item.astype(jnp.bfloat16) for item in qk], axis=1)
        v0 = dot(normed, weight_a(1, s, 0)).astype(jnp.bfloat16)
        v1 = dot(normed, wa[1, s, 1, :, :, :, 0:256].reshape(D_VIS, 256)).astype(jnp.bfloat16)
        vals = dot(jnp.concatenate([v0, v1], axis=1), spread[...]).astype(jnp.bfloat16)
        same = mask[...] > 0
        ctx[...] = jnp.zeros_like(ctx)
        for head in range(HEADS):
            lo = head * HEAD_DIM
            base = lo // 128 * 128
            wide = min(256, WIDTH - base)
            here = (lanes[:, :wide] >= lo - base) & (lanes[:, :wide] < lo - base + HEAD_DIM)
            query = jnp.where(here, qk[:, base : base + wide], jnp.bfloat16(0))
            keys = qk[:, WIDTH + base : WIDTH + base + wide]
            scores = lax.dot_general(
                query, keys, (((1,), (1,)), ((), ())), preferred_element_type=jnp.float32
            ) * HEAD_DIM ** (-0.5)
            scores = jnp.where(same, scores, jnp.float32(-1e30))
            weights = jnp.exp(scores - jnp.max(scores, axis=-1, keepdims=True))
            probs = (weights / jnp.sum(weights, axis=-1, keepdims=True)).astype(jnp.bfloat16)
            lo = head * 2 * HEAD_DIM
            base = lo // 128 * 128
            here = (lanes >= lo - base) & (lanes < lo - base + 2 * HEAD_DIM)
            part = dot(probs, jnp.where(here, vals[:, base : base + 256], jnp.bfloat16(0)))
            ctx[:, base : base + 256] += part
        first = ctx[...]
        second = pltpu.roll(first, 10, 1)
        both = jnp.concatenate([first.astype(jnp.bfloat16), second.astype(jnp.bfloat16)], axis=0)
        o0 = dot(both, wa[1, s, 1, :, :, :, 256:384].reshape(D_VIS, 128))
        o1 = dot(both, weight_b(1, s))
        update = jnp.concatenate(
            [jnp.concatenate([o0[r : r + MB], o1[r : r + MB]], axis=1) for r in (0, MB)], axis=1
        )
        acts[...] = (values + update).astype(jnp.bfloat16)
        return carry

    lax.fori_loop(0, SECTIONS, section, 0)

    final = rms(acts[...].astype(jnp.float32), merge_gain[...])
    for i in range(D_VIS // 128):
        tail[i * MB : (i + 1) * MB, :] = final[:, i * 128 : (i + 1) * 128]
    for j in range(4):
        for i in range(D_VIS // 128):
            rows = tail[pl.ds(i * MB + j, MB // 4, stride=4), :]
            out[:, j * D_VIS + i * 128 : j * D_VIS + (i + 1) * 128] = rows.astype(jnp.bfloat16)


def body(patches, window_ids, norm_gain, w_qkv, w_out, merge_gain):
    core = lax.axis_index("dp") % 2
    count = w_qkv.shape[0]
    qk = w_qkv[:, :, : 2 * WIDTH]
    rows_o = w_out.shape[1]
    halves = jnp.concatenate([w_out[:, :, :WIDTH], w_out[:, :, WIDTH:]], axis=1)
    vo = jnp.concatenate([w_qkv[:, :, 2 * WIDTH :], halves], axis=2)
    swap = [(i, i ^ 1) for i in range(lax.axis_size("dp"))]
    got = lax.ppermute(jnp.where(core == 0, vo, qk), "dp", swap)
    block = jnp.where(
        core == 0, jnp.concatenate([qk, got], axis=1), jnp.concatenate([got, vo], axis=1)
    )
    block_a = jnp.stack([block[:, :, :CA], block[:, :, CA : 2 * CA]], axis=1)
    block_b = block[:, :, 2 * CA :]
    place = jnp.arange(2 * WIDTH)[None, :]
    source = jnp.arange(WIDTH)[:, None]
    spread = ((place % 20 < 10) & (place // 20 * 10 + place % 20 == source)).astype(jnp.bfloat16)
    vmem = pl.BlockSpec(memory_space=pltpu.VMEM)
    hbm = pl.BlockSpec(memory_space=pl.ANY)
    dma = pltpu.SemaphoreType.DMA
    return pl.pallas_call(
        kernel,
        out_shape=jax.ShapeDtypeStruct((MB // 4, 4 * D_VIS), jnp.bfloat16),
        in_specs=[hbm, hbm] + [vmem] * 5,
        out_specs=vmem,
        scratch_shapes=[
            pltpu.VMEM((2, SECTIONS, 2, NX, NY, ROWS, CA), jnp.bfloat16),
            pltpu.VMEM((2, SECTIONS, NX, NY, ROWS, CB), jnp.bfloat16),
            pltpu.VMEM((MB, D_VIS), jnp.bfloat16),
            pltpu.VMEM((MB, 2 * WIDTH), jnp.float32),
            pltpu.VMEM((MB, MB), jnp.float32),
            pltpu.VMEM((D_VIS // 128 * MB, 128), jnp.float32),
            dma((3,)),
            dma((SECTIONS, 3)),
            dma((SECTIONS, 7)),
            dma((SECTIONS, 2)),
            dma((SECTIONS, 7)),
            dma((SECTIONS, 3)),
            dma((SECTIONS,)),
            dma((SECTIONS,)),
            dma((SECTIONS,)),
            dma((8,)),
        ],
        compiler_params=pltpu.CompilerParams(
            collective_id=0, has_side_effects=True, vmem_limit_bytes=60 * 1024 * 1024
        ),
    )(block_a, block_b, patches, window_ids, norm_gain, merge_gain.reshape(1, D_VIS), spread)


def solution(mesh):
    in_specs = (
        P(("dp", "phase"), None),
        P(("dp", "phase"), None),
        P(),
        P(None, "dp", None),
        P(None, "dp", None),
        P(),
    )
    out_specs = P(("dp", "phase"), None)
    return jax.shard_map(body, mesh=mesh, in_specs=in_specs, out_specs=out_specs, check_vma=False)
```

time: 395 us -> 119 us (0.30)
  the two profiles are of different devices: /device:TPU:8 before, /device:TPU:1 now
where the time goes in v1:
time: 119 us; the launch traced here: 118 us
  Pallas kernels  96.9 us (81%)
  starting transfers between devices  12.4 us (10%)
  local copies, waits for them, and re-layouts  6.59 us (6%)
  other arithmetic  2.18 us (2%)
    pallas_call x1, Pallas kernels, body(): pl.pallas_call(kernel, out_shape=jax.ShapeDtypeStruct((MB // 4, 4 * D_VIS...  96.9 us
    ppermute x1, starting transfers between devices, body(): got = lax.ppermute(jnp.where(core == 0, vo, qk), 'dp', swap)  12.4 us
  transfers between devices with their start and end apart: 1, of which 0 were waited for; matrix products, arithmetic and copies ran while one was open for 2% of the time, Pallas kernels for 0%

profile of v1, /device:TPU:1, one launch (start us, length us, event | category | flops | bytes accessed | tf_op | source)
XLA Modules:
  0.0 118.2 jit_solution(4779487231202534252)
XLA Ops:
  0.0 0.9 slice.22
  0.9 1.0 slice.21
  2.0 0.0 copy-start
  2.0 0.9 fusion.11
  2.9 0.1 fusion.10
  3.0 12.4 %collective-permute-start = (bf16[4,20,1280]{2,1,0:T(8,128)(2,1)S(1)}, bf16[4,20,1280]{2,1,0:T(8,128)(2,1)S(1)}, u32[]{:S(2)}, u32[]{:S(2)}) collective-permute-start(bf16[4,20,1280]{2,1,0:T(8,128)(2,1)S(1)} %get-tuple-element.8), channel_id=1, source_target_pairs={{0,12},{12,0},{24,36},{36,24},{48,60},{60,48},{72,84},{84,72},{96,... | collective-permute-start | bytes 614408 | tf_op jit(solution)/shard_map/ppermute | solution.py:247
  15.5 1.8 %fusion.1.spread = bf16[640,1280]{1,0:T(8,128)(2,1)} fusion(s32[1280]{0:T(1024)S(1)} %fusion.3, pred[1280]{0:T(1024)(128)(4,1)S(1)} %fusion.7), kind=kLoop, calls=%fused_computation.2 | loop fusion | flops 2457600 | bytes 1644800 | tf_op jit(solution)/shard_map/convert_element_type | solution.py:255
  17.3 0.0 copy-done
  17.3 0.6 reshape.44.merge_gain
  17.9 0.0 collective-permute-done
  17.9 0.2 maximum_select_fusion
  18.1 0.7 slice.30.block_b
  18.9 0.7 copy.11.block_a
  19.6 96.9 %shard_map.64 = bf16[32,5120]{1,0:T(8,128)(2,1)} custom-call(bf16[4,2,40,384]{3,2,1,0:T(8,128)(2,1)} %copy.11.block_a, bf16[4,40,512]{2,1,0:T(8,128)(2,1)} %slice.30.block_b, bf16[128,1280]{1,0:T(8,128)(2,1)} %patches.1, s32[1,128]{1,0:T(1,128)} %ids.1, f32[4,1280]{1,0:T(4,128)} %gains.1, f32[1,1280]{1,0:T(1,128)} %reshape.44.merge_gain, ...), custom_call_target="tpu_custom_call" | custom-call | tf_op jit(solution)/shard_map/pallas_call | solution.py:259
  116.5 1.7 %copy.19 = bf16[32,5120]{1,0:T(8,128)(2,1)} copy(bf16[32,5120]{1,0:T(8,128)(2,1)} %shard_map.64) | data formatting | bytes 655360
  (7 shorter events, 0.1 us)
Async XLA Ops:
  2.0 15.3 %copy-start = (f32[1280]{0:T(1024)S(1)}, f32[1280]{0:T(1024)}, u32[]{:S(2)}) copy-start(f32[1280]{0:T(1024)} %param.11) | copy-start | bytes 15364
  3.0 14.9 %collective-permute-start = (bf16[4,20,1280]{2,1,0:T(8,128)(2,1)S(1)}, bf16[4,20,1280]{2,1,0:T(8,128)(2,1)S(1)}, u32[]{:S(2)}, u32[]{:S(2)}) collective-permute-start(bf16[4,20,1280]{2,1,0:T(8,128)(2,1)S(1)} %get-tuple-element.8), channel_id=1, source_target_pairs={{0,12},{12,0},{24,36},{36,24},{48,60},{60,48},{72,84},{84,72},{96,... | collective-permute-start | bytes 614408 | tf_op jit(solution)/shard_map/ppermute | solution.py:247

commit v2 on v1

--- a/solution.py
+++ b/solution.py
@@ -24,8 +24,8 @@
 
 
 def kernel(
-    block_a, block_b, patches, ids, gains, merge_gain, spread, out,
-    wa, wb, acts, ctx, mask, tail,
+    block_a, block_b, patches, ids, gains, merge_gain, out,
+    wa, wb, acts, ctx, mask, tail, spread,
     local_sem, ax, ay, az, by, bx, sib_a, sib_z, sib_b, sent,
 ):
     dp, z = lax.axis_index("dp"), lax.axis_index("phase")
@@ -157,21 +157,37 @@
         elif k == 9:
             arrive(wb.at[1 - core, s], sib_b.at[s])
 
-    for tick in range(LAG * (SECTIONS - 1) + STEPS):
+    def tick(t):
         for s in range(SECTIONS):
-            k = tick - LAG * s
+            k = t - LAG * s
             if 0 <= k < STEPS:
                 step_a(s, k)
                 step_b(s, k)
 
-    drain(wa.at[0, :, 0, 0:3, 0], 0)
-    drain(wa.at[0, :, 0, :, 0:7], 1)
-    drain(wa.at[0, :, 0], 2)
-    drain(wa.at[0, :, 0], 3)
-    drain(wa.at[0, :, 0], 4)
-    drain(wb.at[0, :, 0, 0:7], 5)
-    drain(wb.at[0, :, 0:3], 6)
-    drain(wb.at[0], 7)
+    def later(s, t):
+        for j in range(1, SECTIONS):
+            k = t - LAG * j
+
+            @pl.when(s + j < SECTIONS)
+            def _():
+                step_a(s + j, k)
+                step_b(s + j, k)
+
+    tick(0)
+    column = lax.broadcasted_iota(jnp.int32, (1, 2 * WIDTH), 1)
+    inner = lax.rem(column, 20)
+    source = jnp.where(inner < 10, lax.div(column, 20) * 10 + inner, -1)
+
+    def spread_rows(i, carry):
+        row = lax.broadcasted_iota(jnp.int32, (64, 2 * WIDTH), 0) + i * 64
+        spread[pl.ds(pl.multiple_of(i * 64, 64), 64), :] = jnp.where(
+            row == source, jnp.float32(1), jnp.float32(0)
+        ).astype(jnp.bfloat16)
+        return carry
+
+    lax.fori_loop(0, WIDTH // 64, spread_rows, 0)
+    for t in range(1, STEPS):
+        tick(t)
 
     def weight_a(lane, s, h):
         return wa[lane, s, h].reshape(D_VIS, CA)
@@ -194,6 +210,7 @@
         v0 = dot(normed, weight_a(1, s, 0)).astype(jnp.bfloat16)
         v1 = dot(normed, wa[1, s, 1, :, :, :, 0:256].reshape(D_VIS, 256)).astype(jnp.bfloat16)
         vals = dot(jnp.concatenate([v0, v1], axis=1), spread[...]).astype(jnp.bfloat16)
+        later(s, STEPS)
         same = mask[...] > 0
         ctx[...] = jnp.zeros_like(ctx)
         for head in range(HEADS):
@@ -223,9 +240,19 @@
             [jnp.concatenate([o0[r : r + MB], o1[r : r + MB]], axis=1) for r in (0, MB)], axis=1
         )
         acts[...] = (values + update).astype(jnp.bfloat16)
+        later(s, STEPS + 1)
         return carry
 
     lax.fori_loop(0, SECTIONS, section, 0)
+
+    drain(wa.at[0, :, 0, 0:3, 0], 0)
+    drain(wa.at[0, :, 0, :, 0:7], 1)
+    drain(wa.at[0, :, 0], 2)
+    drain(wa.at[0, :, 0], 3)
+    drain(wa.at[0, :, 0], 4)
+    drain(wb.at[0, :, 0, 0:7], 5)
+    drain(wb.at[0, :, 0:3], 6)
+    drain(wb.at[0], 7)
 
     final = rms(acts[...].astype(jnp.float32), merge_gain[...])
     for i in range(D_VIS // 128):
@@ -250,16 +277,13 @@
     )
     block_a = jnp.stack([block[:, :, :CA], block[:, :, CA : 2 * CA]], axis=1)
     block_b = block[:, :, 2 * CA :]
-    place = jnp.arange(2 * WIDTH)[None, :]
-    source = jnp.arange(WIDTH)[:, None]
-    spread = ((place % 20 < 10) & (place // 20 * 10 + place % 20 == source)).astype(jnp.bfloat16)
     vmem = pl.BlockSpec(memory_space=pltpu.VMEM)
     hbm = pl.BlockSpec(memory_space=pl.ANY)
     dma = pltpu.SemaphoreType.DMA
     return pl.pallas_call(
         kernel,
         out_shape=jax.ShapeDtypeStruct((MB // 4, 4 * D_VIS), jnp.bfloat16),
-        in_specs=[hbm, hbm] + [vmem] * 5,
+        in_specs=[hbm, hbm] + [vmem] * 4,
         out_specs=vmem,
         scratch_shapes=[
             pltpu.VMEM((2, SECTIONS, 2, NX, NY, ROWS, CA), jnp.bfloat16),
@@ -268,6 +292,7 @@
             pltpu.VMEM((MB, 2 * WIDTH), jnp.float32),
             pltpu.VMEM((MB, MB), jnp.float32),
             pltpu.VMEM((D_VIS // 128 * MB, 128), jnp.float32),
+            pltpu.VMEM((WIDTH, 2 * WIDTH), jnp.bfloat16),
             dma((3,)),
             dma((SECTIONS, 3)),
             dma((SECTIONS, 7)),
@@ -282,7 +307,7 @@
         compiler_params=pltpu.CompilerParams(
             collective_id=0, has_side_effects=True, vmem_limit_bytes=60 * 1024 * 1024
         ),
-    )(block_a, block_b, patches, window_ids, norm_gain, merge_gain.reshape(1, D_VIS), spread)
+    )(block_a, block_b, patches, window_ids, norm_gain, merge_gain.reshape(1, D_VIS))
 
 
 def solution(mesh):

time: 119 us -> 106 us (0.89)
  Pallas kernels: 96.9 us -> 86.7 us
  other arithmetic: 2.18 us -> 0.34 us
    pallas_call x1, Pallas kernels: 96.9 us -> 86.7 us  [body(): pl.pallas_call(kernel, out_shape=jax.ShapeDtypeStruct((MB // 4, 4 * D_VIS...]
    convert_element_type x1 -> x0, other arithmetic: 1.81 us -> none  [body(): ((place % 20 < 10) & (place // 20 * 10 + place % 20 == source)).astype(jn...]
    unnamed x6 -> x8, local copies, waits for them, and re-layouts: 1.77 us -> 2.66 us
  transfers between devices with their start and end apart: 1 -> 1, of which waited for: 0 -> 1; matrix products, arithmetic and copies ran while one was open for 2% -> 1% of each run, Pallas kernels for 0% -> 0%
where the time goes in v2:
time: 106 us
  Pallas kernels  86.7 us (82%)
  starting transfers between devices  12.4 us (12%)
  local copies, waits for them, and re-layouts  5.61 us (5%)
    pallas_call x1, Pallas kernels, body(): pl.pallas_call(kernel, out_shape=jax.ShapeDtypeStruct((MB // 4, 4 * D_VIS...  86.7 us
    ppermute x1, starting transfers between devices, body(): got = lax.ppermute(jnp.where(core == 0, vo, qk), 'dp', swap)  12.4 us
    unnamed x8, local copies, waits for them, and re-layouts  2.66 us
  transfers between devices with their start and end apart: 1, of which 1 were waited for; matrix products, arithmetic and copies ran while one was open for 1% of the time, Pallas kernels for 0%

profile of v2, /device:TPU:1, one launch (start us, length us, event | category | flops | bytes accessed | tf_op | source)
XLA Modules:
  0.0 105.7 jit_solution(8724847071386891459)
XLA Ops:
  0.0 0.0 copy-start
  0.0 0.9 copy-done
  0.9 0.0 slice-start
  1.0 0.0 slice-start.1
  1.0 0.8 slice-done
  1.9 0.1 slice-done.1
  1.9 0.0 copy-start.1
  1.9 0.1 fusion
  2.0 12.4 %collective-permute-start = (bf16[4,20,1280]{2,1,0:T(8,128)(2,1)S(1)}, bf16[4,20,1280]{2,1,0:T(8,128)(2,1)S(1)}, u32[]{:S(2)}, u32[]{:S(2)}) collective-permute-start(bf16[4,20,1280]{2,1,0:T(8,128)(2,1)S(1)} %get-tuple-element.8), channel_id=1, source_target_pairs={{0,12},{12,0},{24,36},{36,24},{48,60},{60,48},{72,84},{84,72},{96,... | collective-permute-start | bytes 614408 | tf_op jit(solution)/shard_map/ppermute | solution.py:274
  14.5 0.0 copy-done.1
  14.5 0.6 reshape.3.merge_gain
  15.0 0.5 collective-permute-done
  15.6 0.2 maximum_select_fusion
  15.8 0.7 slice.30.block_b
  16.5 0.7 copy.11.block_a
  17.3 86.7 %shard_map.64 = bf16[32,5120]{1,0:T(8,128)(2,1)} custom-call(bf16[4,2,40,384]{3,2,1,0:T(8,128)(2,1)} %copy.11.block_a, bf16[4,40,512]{2,1,0:T(8,128)(2,1)} %slice.30.block_b, bf16[128,1280]{1,0:T(8,128)(2,1)} %patches.1, s32[1,128]{1,0:T(1,128)} %ids.1, f32[4,1280]{1,0:T(4,128)} %gains.1, f32[1,1280]{1,0:T(1,128)} %reshape.3.merge_gain), custom_call_target="tpu_custom_call" | custom-call | tf_op jit(solution)/shard_map/pallas_call | solution.py:283
  104.0 1.7 %copy.19 = bf16[32,5120]{1,0:T(8,128)(2,1)} copy(bf16[32,5120]{1,0:T(8,128)(2,1)} %shard_map.64) | data formatting | bytes 655360
  (6 shorter events, 0.1 us)
Async XLA Ops:
  0.0 0.9 copy-start
  0.9 0.9 slice-start
  1.0 1.0 slice-start.1
  1.9 12.5 %copy-start.1 = (f32[1280]{0:T(1024)S(1)}, f32[1280]{0:T(1024)}, u32[]{:S(2)}) copy-start(f32[1280]{0:T(1024)} %param.11) | copy-start | bytes 15364
  2.0 13.5 %collective-permute-start = (bf16[4,20,1280]{2,1,0:T(8,128)(2,1)S(1)}, bf16[4,20,1280]{2,1,0:T(8,128)(2,1)S(1)}, u32[]{:S(2)}, u32[]{:S(2)}) collective-permute-start(bf16[4,20,1280]{2,1,0:T(8,128)(2,1)S(1)} %get-tuple-element.8), channel_id=1, source_target_pairs={{0,12},{12,0},{24,36},{36,24},{48,60},{60,48},{72,84},{84,72},{96,... | collective-permute-start | bytes 614408 | tf_op jit(solution)/shard_map/ppermute | solution.py:274
